TPU v7x, 256 devices: a whole 4x4x8 slice. The times are simulated.
256 devices in a mesh: tm: 32 (over x, y, core), ens: 8 (over z).
Axes of the slice: x: 4, y: 4, z: 8, core: 2. Of those that a mesh axis runs over, the one named last changes fastest.
Arguments:
- propagators: float32 [8, 32, 512, 512], P('ens', 'tm'), may hold values from -1 to 1, as said below
- weights: float32 [8], P('ens'), may hold values from 2 to 8
- target: float32 [512, 512], replicated, may hold values from -1 to 1, as said below
Outputs:
- gradient: float32 [512, 32, 512], P('ens', 'tm')
Inputs may be any that keep to these rules, and one draw needn't show every extreme that they name: Every propagators[m, t] is an orthogonal 512 x 512 matrix up to float32 rounding. target is an orthogonal 512 x 512 matrix up to float32 rounding.
All inputs are finite; a program needn't handle non-finite values.
Results may differ from a plain program's by a relative error of at most 0.0003.
Values sent between devices are 32-bit elements; how exact they have to be, the bound alone decides.
A program may use at most 128 MiB of HBM per device.

v0:
```python
import jax
import jax.numpy as jnp
from jax import lax
from jax.sharding import PartitionSpec as P

highest = lax.Precision.HIGHEST


def carried_in(part, axis, combine, identity):
    place = lax.axis_index(axis)
    gathered = lax.all_gather(part, axis)
    state = jnp.zeros_like(part) + jnp.asarray(identity, part.dtype)

    def one(lap, state):
        return combine(state, lax.dynamic_index_in_dim(gathered, lap, 0, False))

    return lax.fori_loop(0, place, one, state)


def spread(value, axis, root):
    mine = lax.axis_index(axis) == root
    return lax.psum(jnp.where(mine, value, jnp.zeros_like(value)), axis)


def multiply(left_side, right_side):
    return jnp.einsum("mij,mjk->mik", left_side, right_side, precision=highest)


def compose_forward(earlier, later):
    return multiply(later, earlier)


def shards(propagators, weights, target):
    slices = propagators.shape[1]
    order = target.shape[0]
    block_product = propagators[:, 0]
    identity = jnp.broadcast_to(jnp.eye(order, dtype=jnp.float32), block_product.shape)
    before = carried_in(block_product, "tm", compose_forward, identity)
    running = before
    running = multiply(propagators[:, 0], running)
    collected = [running]
    stacked = jnp.stack(collected, axis=1)
    last_prefix = stacked[:, slices - 1]
    final_product = spread(last_prefix, "tm", lax.axis_size("tm") - 1)
    twisted = jnp.einsum("ki,mkj->mij", target, final_product, precision=highest)
    skew_part = weights[:, None, None] * (twisted - jnp.swapaxes(twisted, 1, 2)) * 0.5
    right_factor = jnp.einsum("mij,mtkj->mtik", skew_part, stacked, precision=highest)
    return lax.psum_scatter(
        jnp.einsum("mtik,mtkj->itj", stacked, right_factor, precision=highest),
        "ens",
        scatter_dimension=0,
        tiled=True,
    )


def solution(mesh):
    placed = (P("ens", "tm", None, None), P("ens"), P())
    return jax.shard_map(
        shards, mesh=mesh, in_specs=placed, out_specs=P("ens", "tm", None), check_vma=False
    )
```

profile of v0, /device:TPU:2, one launch (start us, length us, event | category | flops | bytes accessed | tf_op | source)
XLA Modules:
  0.0 447.1 jit_solution(15036979733809586489)
XLA Ops:
  6.5 0.0 copy-start
  6.5 0.0 copy-start.1
  6.5 0.0 all-gather.2.cloned.1.call-start
  6.5 0.7 all-gather.2.cloned.1.call-update
  7.3 0.0 all-reduce.4.cloned.1.call-start
  7.3 0.1 fusion.11
  7.4 124.1 %all-gather.2.cloned.1.call-done = f32[32,1,512,512]{3,2,1,0:T(8,128)} async-done(((f32[1,1,512,512]{3,2,1,0:T(8,128)}), f32[32,1,512,512]{3,2,1,0:T(8,128)}) %all-gather.2.cloned.1.call-update) | async-done | bytes 33554448 | tf_op jit(solution)/shard_map/all_gather | solution.py:11
  131.6 25.4 %while.10 = (s32[]{:T(128)}, f32[1,512,512]{2,1,0:T(8,128)S(1)}, s32[]{:T(128)}, f32[32,1,512,512]{3,2,1,0:T(8,128)}, s32[]{:T(128)}, /*index=5*/s32[]{:T(128)}, s32[]{:T(128)}) while((s32[]{:T(128)}, f32[1,512,512]{2,1,0:T(8,128)S(1)}, s32[]{:T(128)}, f32[32,1,512,512]{3,2,1,0:T(8,128)}, s32[]{:T(128)}, /*index=5*/s32[]{:T(128)}, ...), condition=%wide.region_1.2_spmd, body=%wide.region_0.1_spmd.sunk | while | flops 1610612736 | bytes 5242995 | solution.py:17
  131.6 0.1 copy.18
  131.6 3.1 convolution_bitcast_fusion.5
  134.7 0.1 copy.18
  134.8 3.1 convolution_bitcast_fusion.5
  137.9 0.1 copy.18
  138.0 3.1 convolution_bitcast_fusion.5
  141.1 0.1 copy.18
  141.2 3.1 convolution_bitcast_fusion.5
  144.3 0.1 copy.18
  144.3 3.1 convolution_bitcast_fusion.5
  147.4 0.1 copy.18
  147.5 3.1 convolution_bitcast_fusion.5
  150.6 0.1 copy.18
  150.7 3.1 convolution_bitcast_fusion.5
  153.8 0.1 copy.18
  153.9 3.1 convolution_bitcast_fusion.5
  157.0 4.7 %fusion.8 = f32[512,512]{1,0:T(8,128)S(1)} fusion(f32[1,1,512,512]{3,2,1,0:T(8,128)} %param.5, f32[1,512,512]{2,1,0:T(8,128)S(1)} %get-tuple-element.28), kind=kOutput, calls=%fused_computation.12 | convolution fusion | flops 1610612736 | bytes 3145728 | tf_op jit(solution)/shard_map/mij,mjk->mik/dot_general | solution.py:26
  161.7 1.1 select_bitcast_fusion
  162.8 0.0 all-reduce.4.cloned.1.call-update
  162.8 0.2 all-reduce.6.cloned.1.call-start
  163.7 185.9 %all-reduce.4.cloned.1.call-done = f32[512,512]{0,1:T(8,128)} async-done(((f32[512,512]{0,1:T(8,128)}), f32[512,512]{0,1:T(8,128)}) %all-reduce.4.cloned.1.call-update) | async-done | bytes 1048592 | tf_op jit(solution)/shard_map/psum | solution.py:22
  349.6 0.0 copy-done
  349.6 3.1 convolution_bitcast_fusion.3
  352.7 1.3 copy.6
  354.0 4.7 %convolution_bitcast_fusion.2 = f32[512,512]{0,1:T(8,128)S(1)} fusion(f32[512,512]{1,0:T(8,128)S(1)} %fusion.8, f32[1,512,512]{2,1,0:T(8,128)S(1)} %convolution_bitcast_fusion.3, f32[1,512,512]{1,2,0:T(8,128)} %copy.6, f32[]{:T(128)} %bitcast.53), kind=kOutput, calls=%fused_computation.6 | convolution fusion | flops 1611399168 | bytes 4194308 | tf_op jit(solution)/shard_map/mij,mtkj->mtik/dot_general | solution.py:47
  358.7 1.8 convolution_bitcast_fusion.1
  360.5 2.0 copy.7
  362.5 0.0 all-reduce.6.cloned.1.call-update
  362.5 0.0 copy-done.1
  362.5 0.6 dynamic-slice
  363.8 75.2 %all-reduce.6.cloned.1.call-done = f32[512,1,512]{2,1,0:T(1,128)} async-done(((f32[512,1,512]{2,1,0:T(1,128)}), f32[512,1,512]{2,1,0:T(1,128)}) %all-reduce.6.cloned.1.call-update) | async-done | bytes 1048592
  439.0 1.6 constant_dynamic-slice_fusion
Async XLA Ops:
  6.5 343.1 %copy-start = (f32[512,512]{1,0:T(8,128)S(1)}, f32[512,512]{1,0:T(8,128)}, u32[]{:S(2)}) copy-start(f32[512,512]{1,0:T(8,128)} %param.7) | copy-start | bytes 3145732
  6.5 356.0 %copy-start.1 = (u32[256]{0:T(256)S(1)}, u32[256]{0:T(256)}, u32[]{:S(2)}) copy-start(u32[256]{0:T(256)} %constant.26) | copy-start | bytes 3076
  6.5 125.0 %all-gather.2.cloned.1.call-start = ((), (), s32[]{:S(2)}) async-start(), calls=%async_computation | async-start | bytes 34603008 | tf_op jit(solution)/shard_map/all_gather | solution.py:11
  7.3 342.3 %all-reduce.4.cloned.1.call-start = ((), (), s32[]{:S(2)}) async-start(), calls=%async_computation.1 | async-start | bytes 2097152 | tf_op jit(solution)/shard_map/psum | solution.py:22
  162.8 276.2 %all-reduce.6.cloned.1.call-start = ((), (), s32[]{:S(2)}) async-start(), calls=%async_computation.2 | async-start | bytes 2097152
Sparse Core Ops, SparseCore 0:
  9.9 121.6 all-gather.1
  162.9 186.6 all-reduce.3
  362.6 76.3 all-reduce.5
where the time goes:
time: 449 us; the launch traced here: 447 us
  waiting for transfers between devices  386 us (86%)
  matrix products  38.8 us (9%)
  between operations  14.5 us (3%)
  local copies, waits for them, and re-layouts  5.98 us (1%)
    psum x1, waiting for transfers between devices, spread(): return lax.psum(jnp.where(mine, value, jnp.zeros_like(value)), axis)  186 us
    all_gather x1, waiting for transfers between devices, carried_in(): gathered = lax.all_gather(part, axis)  124 us
    unnamed x4, waiting for transfers between devices  76 us
    dot_general x9, matrix products, multiply(): return jnp.einsum('mij,mjk->mik', left_side, right_side, precision=highest)  29.2 us
  transfers between devices with their start and end apart: 3, of which 3 were waited for; matrix products, arithmetic and copies ran while one was open for 0% of the time, Pallas kernels for 0%

commit v1 on v0

--- a/solution.py
+++ b/solution.py
@@ -19,7 +19,7 @@
 
 def spread(value, axis, root):
     mine = lax.axis_index(axis) == root
-    return lax.psum(jnp.where(mine, value, jnp.zeros_like(value)), axis)
+    return jnp.sum(lax.all_gather(jnp.where(mine, value, jnp.zeros_like(value)), axis), axis=0)
 
 
 def multiply(left_side, right_side):

time: 449 us -> 488 us (1.087)
  local copies, waits for them, and re-layouts: 5.98 us -> 38.5 us
  other arithmetic: 1.24 us -> 6.54 us
    all_gather x0 -> x1, waiting for transfers between devices: none -> 190 us  [spread(): lax.all_gather(jnp.where(mine, value, jnp.zeros_like(value)), axis)]
    psum x1 -> x0, waiting for transfers between devices: 186 us -> none  [spread(): return lax.psum(jnp.where(mine, value, jnp.zeros_like(value)), axis)]
    unnamed x6 -> x7, local copies, waits for them, and re-layouts: 2.16 us -> 34.7 us
    reduce_sum x0 -> x1, other arithmetic: none -> 5.36 us  [spread(): jnp.sum(lax.all_gather(jnp.where(mine, value, jnp.zeros_like(value)), axi...]
where the time goes in v1:
time: 488 us; the launch traced here: 487 us
  waiting for transfers between devices  389 us (80%)
  local copies, waits for them, and re-layouts  38.5 us (8%)
  matrix products  37.6 us (8%)
  between operations  14.5 us (3%)
  other arithmetic  6.54 us (1%)
    all_gather x1, waiting for transfers between devices, spread(): lax.all_gather(jnp.where(mine, value, jnp.zeros_like(value)), axis)  190 us
    all_gather x1, waiting for transfers between devices, carried_in(): gathered = lax.all_gather(part, axis)  124 us
    unnamed x4, waiting for transfers between devices  75 us
    unnamed x7, local copies, waits for them, and re-layouts  34.7 us
    dot_general x9, matrix products, multiply(): return jnp.einsum('mij,mjk->mik', left_side, right_side, precision=highest)  29.2 us
  transfers between devices with their start and end apart: 3, of which 3 were waited for; matrix products, arithmetic and copies ran while one was open for 0% of the time, Pallas kernels for 0%

profile of v1, /device:TPU:2, one launch (start us, length us, event | category | flops | bytes accessed | tf_op | source)
XLA Modules:
  0.0 486.7 jit_solution(17153444701958856111)
XLA Ops:
  6.5 0.0 copy-start
  6.5 0.0 all-gather.4.cloned.1.call-start
  6.5 0.7 all-gather.4.cloned.1.call-update
  7.3 0.0 all-gather.6.cloned.1.call-start
  7.3 0.1 fusion.11
  7.4 124.1 %all-gather.4.cloned.1.call-done = f32[32,1,512,512]{3,2,1,0:T(8,128)} async-done(((f32[1,1,512,512]{3,2,1,0:T(8,128)}), f32[32,1,512,512]{3,2,1,0:T(8,128)}) %all-gather.4.cloned.1.call-update) | async-done | bytes 33554448 | tf_op jit(solution)/shard_map/all_gather | solution.py:11
  131.6 25.4 %while.10 = (s32[]{:T(128)}, f32[1,512,512]{2,1,0:T(8,128)S(1)}, s32[]{:T(128)}, f32[32,1,512,512]{3,2,1,0:T(8,128)}, s32[]{:T(128)}, /*index=5*/s32[]{:T(128)}, s32[]{:T(128)}) while((s32[]{:T(128)}, f32[1,512,512]{2,1,0:T(8,128)S(1)}, s32[]{:T(128)}, f32[32,1,512,512]{3,2,1,0:T(8,128)}, s32[]{:T(128)}, /*index=5*/s32[]{:T(128)}, ...), condition=%wide.region_1.2_spmd, body=%wide.region_0.1_spmd.sunk | while | flops 1610612736 | bytes 5242995 | solution.py:17
  131.6 0.1 copy.18
  131.6 3.1 convolution_bitcast_fusion.5
  134.7 0.1 copy.18
  134.8 3.1 convolution_bitcast_fusion.5
  137.9 0.1 copy.18
  138.0 3.1 convolution_bitcast_fusion.5
  141.1 0.1 copy.18
  141.2 3.1 convolution_bitcast_fusion.5
  144.3 0.1 copy.18
  144.3 3.1 convolution_bitcast_fusion.5
  147.4 0.1 copy.18
  147.5 3.1 convolution_bitcast_fusion.5
  150.6 0.1 copy.18
  150.7 3.1 convolution_bitcast_fusion.5
  153.8 0.1 copy.18
  153.9 3.1 convolution_bitcast_fusion.5
  157.0 4.7 fusion.8
  161.7 1.1 select_bitcast_fusion
  162.7 0.0 all-gather.6.cloned.1.call-update
  162.8 0.2 all-reduce.3.cloned.1.call-start
  163.6 189.8 %all-gather.6.cloned.1.call-done = f32[16384,512]{0,1:T(8,128)} async-done(((f32[512,512]{0,1:T(8,128)}), f32[16384,512]{0,1:T(8,128)}) %all-gather.6.cloned.1.call-update) | async-done | bytes 33554448 | tf_op jit(solution)/shard_map/all_gather | solution.py:22
  353.4 32.5 %copy.8 = f32[64,8,32,512]{3,2,1,0:T(8,128)S(1)} copy(f32[64,8,32,512]{3,1,2,0:T(8,128)} %bitcast.59) | data formatting | bytes 67108864
  385.9 0.0 copy-start.1
  386.0 5.4 %bitcast_reduce_fusion = f32[512,512]{0,1:T(8,128)S(1)} fusion(f32[64,8,32,512]{3,2,1,0:T(8,128)S(1)} %copy.8), kind=kLoop, calls=%fused_computation.5 | loop fusion | flops 8126464 | bytes 34603008 | tf_op jit(solution)/shard_map/reduce_sum | solution.py:22
  391.3 0.0 copy-done
  391.3 1.9 convolution_bitcast_fusion.3
  393.2 1.3 copy.6
  394.5 4.7 convolution_bitcast_fusion.2
  399.2 1.8 convolution_bitcast_fusion.1
  401.1 2.0 copy.7
  403.0 0.0 all-reduce.3.cloned.1.call-update
  403.0 0.0 copy-done.1
  403.0 0.6 dynamic-slice
  404.3 74.3 %all-reduce.3.cloned.1.call-done = f32[512,1,512]{2,1,0:T(1,128)} async-done(((f32[512,1,512]{2,1,0:T(1,128)}), f32[512,1,512]{2,1,0:T(1,128)}) %all-reduce.3.cloned.1.call-update) | async-done | bytes 1048592
  478.6 1.6 constant_dynamic-slice_fusion
Async XLA Ops:
  6.5 384.8 %copy-start = (f32[512,512]{1,0:T(8,128)S(1)}, f32[512,512]{1,0:T(8,128)}, u32[]{:S(2)}) copy-start(f32[512,512]{1,0:T(8,128)} %param.7) | copy-start | bytes 3145732
  6.5 125.0 %all-gather.4.cloned.1.call-start = ((), (), s32[]{:S(2)}) async-start(), calls=%async_computation | async-start | bytes 34603008 | tf_op jit(solution)/shard_map/all_gather | solution.py:11
  7.3 346.2 %all-gather.6.cloned.1.call-start = ((), (), s32[]{:S(2)}) async-start(), calls=%async_computation.1 | async-start | bytes 34603008 | tf_op jit(solution)/shard_map/all_gather | solution.py:22
  162.8 315.8 %all-reduce.3.cloned.1.call-start = ((), (), s32[]{:S(2)}) async-start(), calls=%async_computation.2 | async-start | bytes 2097152
  385.9 17.1 %copy-start.1 = (u32[256]{0:T(256)S(1)}, u32[256]{0:T(256)}, u32[]{:S(2)}) copy-start(u32[256]{0:T(256)} %constant.27) | copy-start | bytes 3076
Sparse Core Ops, SparseCore 0:
  9.9 121.6 all-gather.3
  162.9 190.4 all-gather.5
  403.2 75.3 all-reduce.2
